TPU v7x, 32 devices: a whole 2x2x4 slice. The times are simulated.
32 devices in a mesh: leaf: 2 (over x), row: 4 (over y, core), col: 4 (over z).
Axes of the slice: x: 2, y: 2, z: 4, core: 2. Of those that a mesh axis runs over, the one named last changes fastest.
Arguments:
- leaf_front: float32 [2, 7, 4, 128, 7, 4, 128], P('leaf', None, 'row', None, None, 'col')
- leaf_pattern: int32 [2, 28, 28], P('leaf'), may hold values from 0 to 1, as said below
- parent_panel: float32 [1, 2, 7, 4, 128, 4, 128], P(None, 'leaf', None, 'row', None, 'col'), may hold values from -0.125 to 0.125
- parent_diag: float32 [1, 2, 7, 4, 128], P(None, 'leaf', None, 'row'), may hold values from 1.5 to 2.5
- parent_pattern: int32 [1, 2, 28, 28], replicated, may hold values from 0 to 1, as said below
- ext_map: int32 [1, 2, 24], replicated, may hold values from 0 to 27, as said below
Outputs:
- panels: float32 [2, 2, 7, 4, 128, 4, 128], P(None, 'leaf', None, 'row', None, 'col')
- top_update: float32 [2, 6, 4, 128, 6, 4, 128], P('leaf', None, 'row', None, None, 'col')
Inputs may be any that keep to these rules, and one draw needn't show every extreme that they name: leaf_pattern: symmetric, with every diagonal block 1. parent_pattern: symmetric, with every diagonal block 1. parent_pattern[d, n] belongs to node n at depth d+1; rows n of 2 / 2^(d+1) or more are not read. ext_map[d, n] belongs to node n at depth d; rows n of 2 / 2^d or more are not read. Along its 24 entries it rises strictly; ext_map[d, n, j] - j is the same for the 4 entries j of each aligned run of 4, never falls and lies in 0 to 4. Among the entries j of one class of j mod 4, at most two lie in one class of ext_map mod 4, and in every row some two do.
All inputs are finite; a program needn't handle non-finite values.
Results may differ from a plain program's by a relative error of at most 0.0003.
Values sent between devices are 32-bit elements; how exact they have to be, the bound alone decides.
A program may use at most 128 MiB of HBM per device.

v0:
```python
import jax
import jax.numpy as jnp
from jax import lax
from jax.sharding import PartitionSpec as P

highest = lax.Precision.HIGHEST
slot_limit = 2


def from_root(value, axis, source):
    kept = jnp.where(lax.axis_index(axis) == source, value, 0).astype(value.dtype)
    return lax.psum(kept, axis)


def partner_2(block, axis, bit):
    count = lax.axis_size(axis)
    route = []
    for low in range(count):
        high = low | 1 << bit
        if high != low and high < count:
            route += [(low, high), (high, low)]
    return lax.ppermute(block, axis, route)


def symmetric_lower(matrix):
    return jnp.tril(matrix) + jnp.tril(matrix, -1).T


def local_mask(pattern, my_row, my_col, block_rows, grid_side):
    layout = pattern.reshape(block_rows, grid_side, block_rows, grid_side).astype(jnp.float32)
    picked = lax.dynamic_index_in_dim(layout, my_row, 1, keepdims=False)
    picked = lax.dynamic_index_in_dim(picked, my_col, 2, keepdims=False)
    return picked[:, None, :, None]


def factor_whole(front_local, my_row, my_col, grid_side, block_size, kept):
    local_order = front_local.shape[0]
    block_rows = local_order // block_size
    pivots = grid_side * block_size
    squares = lax.all_gather(
        front_local[None, :block_size, :block_size], ("row", "col"), axis=0, tiled=True
    )
    corner = (
        squares.reshape(grid_side, grid_side, block_size, block_size)
        .transpose(0, 2, 1, 3)
        .reshape(pivots, pivots)
    )
    pivot_wide = lax.all_gather(front_local[:, :block_size], "col", axis=1, tiled=True)
    pivot_factor = jnp.linalg.cholesky(symmetric_lower(corner))
    solved = lax.linalg.triangular_solve(
        pivot_factor, pivot_wide[block_size:], left_side=False, lower=True, transpose_a=True
    )
    top_rows = lax.dynamic_slice(pivot_factor, (my_row * block_size, 0), (block_size, pivots))
    rows_here = jnp.concatenate([top_rows, solved], axis=0)
    rows_there = from_root(rows_here, "row", my_col)
    picked_rows = jnp.take(
        rows_there.reshape(block_rows, block_size, pivots), kept, axis=0
    ).reshape(-1, pivots)
    panel_col = lax.dynamic_slice(rows_here, (0, my_col * block_size), (local_order, block_size))
    update = front_local[block_size:, block_size:] - jnp.einsum(
        "ik,jk->ij",
        rows_here[block_size:],
        picked_rows[block_size:],
        precision=highest,
        preferred_element_type=jnp.float32,
    )
    return (panel_col, update)


def factor(front_local, my_row, my_col, grid_side, block_size, kept):
    return factor_whole(front_local, my_row, my_col, grid_side, block_size, kept)


def route_tables(child_map, grid_side, my_index, block_rows):
    layout = child_map.reshape(-1, grid_side)
    row_total = layout.shape[0]
    target = layout % grid_side
    home_row = layout // grid_side
    order_ids = jnp.arange(row_total)
    before = order_ids[:, None] > order_ids[None, :]
    shared = target[:, None, :] == target[None, :, :]
    position = jnp.sum(jnp.logical_and(shared, before[:, :, None]).astype(jnp.int32), axis=1)
    own_target = lax.dynamic_index_in_dim(target, my_index, 1, keepdims=False)
    own_position = lax.dynamic_index_in_dim(position, my_index, 1, keepdims=False)
    slot_ids = jnp.arange(slot_limit)
    side_ids = jnp.arange(grid_side)
    outgoing = jnp.logical_and(
        own_target[None, None, :] == side_ids[:, None, None],
        own_position[None, None, :] == slot_ids[None, :, None],
    ).astype(jnp.int32)
    send_index = jnp.sum(outgoing * order_ids[None, None, :], axis=2).reshape(-1)
    send_valid = jnp.sum(outgoing, axis=2).reshape(-1).astype(jnp.float32)
    matches = (
        (target == my_index)[:, :, None, None]
        & (position[:, :, None, None] == slot_ids[None, None, :, None])
        & (home_row[:, :, None, None] == jnp.arange(block_rows)[None, None, None, :])
    )
    incoming = jnp.sum(matches.astype(jnp.int32), axis=0)
    flat_ids = side_ids[:, None] * slot_limit + slot_ids[None, :]
    place_index = jnp.sum(incoming * flat_ids[:, :, None], axis=(0, 1))
    place_valid = jnp.sum(incoming, axis=(0, 1)).astype(jnp.float32)
    return (send_index, send_valid, place_index, place_valid)


def shards(leaf_front, leaf_pattern, parent_panel, parent_diag, parent_pattern, ext_map):
    block_rows = leaf_front.shape[1]
    block_size = leaf_front.shape[3]
    local_order = block_rows * block_size
    contrib_rows = block_rows - 1
    levels = parent_panel.shape[0]
    grid_side = lax.axis_size("row")
    my_row = lax.axis_index("row")
    my_col = lax.axis_index("col")
    my_leaf = lax.axis_index("leaf")
    all_blocks = jnp.arange(block_rows, dtype=jnp.int32)
    leaf_local = leaf_front[0, :, 0, :, :, 0, :]
    front_local = (
        leaf_local * local_mask(leaf_pattern[0], my_row, my_col, block_rows, grid_side)
    ).reshape(local_order, local_order)
    panel_col, update = factor(front_local, my_row, my_col, grid_side, block_size, all_blocks)
    panel_list = [panel_col]
    acc_panel = parent_panel.reshape(levels, block_rows, block_size, block_size)
    acc_diag = parent_diag.reshape(levels, block_rows, block_size)
    block_same = (
        jnp.arange(block_rows)[:, None, None, None] == jnp.arange(block_rows)[None, None, :, None]
    )
    element_same = (
        jnp.arange(block_size)[None, :, None, None] == jnp.arange(block_size)[None, None, None, :]
    )
    diag_spots = jnp.logical_and(jnp.logical_and(block_same, element_same), my_row == my_col)
    for depth in range(levels):
        child_node = jnp.right_shift(my_leaf, depth)
        child_map = lax.dynamic_index_in_dim(ext_map[depth], child_node, 0, keepdims=False)
        row_src, row_ok, row_place, row_in = route_tables(child_map, grid_side, my_row, block_rows)
        col_src, col_ok, col_place, col_in = route_tables(child_map, grid_side, my_col, block_rows)
        update_blocks = update.reshape(contrib_rows, block_size, contrib_rows, block_size)
        rows_taken = jnp.take(update_blocks, row_src, axis=0) * row_ok[:, None, None, None]
        packed = jnp.take(rows_taken, col_src, axis=2) * col_ok[None, None, :, None]
        packed = packed.reshape(
            grid_side, slot_limit, block_size, grid_side, slot_limit, block_size
        )
        packed = packed.transpose(0, 3, 1, 4, 2, 5).reshape(
            grid_side * grid_side, slot_limit * slot_limit, block_size, block_size
        )
        received = lax.all_to_all(packed, ("row", "col"), split_axis=0, concat_axis=0, tiled=True)
        received = received.reshape(
            grid_side, grid_side, slot_limit, slot_limit, block_size, block_size
        )
        received = received.transpose(0, 2, 1, 3, 4, 5).reshape(
            grid_side * slot_limit, grid_side * slot_limit, block_size, block_size
        )
        placed = jnp.take(received, row_place, axis=0)
        placed = jnp.take(placed, col_place, axis=1)
        placed = placed * (row_in[:, None, None, None] * col_in[None, :, None, None])
        spread = placed.transpose(0, 2, 1, 3)
        parent_node = jnp.right_shift(my_leaf, depth + 1)
        pattern = lax.dynamic_index_in_dim(parent_pattern[depth], parent_node, 0, keepdims=False)
        mask_here = local_mask(pattern, my_row, my_col, block_rows, grid_side)
        own_front = spread + jnp.where(
            diag_spots, acc_diag[depth][:, :, None, None] * mask_here, 0.0
        )
        own_front = own_front.at[:, :, 0, :].add(mask_here[:, :, 0, :] * acc_panel[depth])
        if depth + 1 < levels:
            partner, partner_panel, partner_diag = partner_2(
                (own_front, acc_panel[depth + 1 :], acc_diag[depth + 1 :]), "leaf", depth
            )
            acc_panel = jnp.concatenate(
                [acc_panel[: depth + 1], acc_panel[depth + 1 :] + partner_panel], axis=0
            )
            acc_diag = jnp.concatenate(
                [acc_diag[: depth + 1], acc_diag[depth + 1 :] + partner_diag], axis=0
            )
        else:
            partner = partner_2(own_front, "leaf", depth)
        front_local = (own_front + partner).reshape(local_order, local_order)
        panel_col, update = factor(front_local, my_row, my_col, grid_side, block_size, all_blocks)
        panel_list.append(panel_col)
    panels = jnp.stack(panel_list).reshape(levels + 1, 1, block_rows, 1, block_size, 1, block_size)
    element_ids = jnp.arange(block_size)
    row_ids = (grid_side * (jnp.arange(contrib_rows) + 1) + my_row)[
        :, None
    ] * block_size + element_ids[None, :]
    col_ids = (grid_side * (jnp.arange(contrib_rows) + 1) + my_col)[
        :, None
    ] * block_size + element_ids[None, :]
    keep_lower = row_ids[:, :, None, None] >= col_ids[None, None, :, :]
    top_rows = jnp.where(
        keep_lower, update.reshape(contrib_rows, block_size, contrib_rows, block_size), 0.0
    )
    top_update = top_rows.reshape(1, contrib_rows, 1, block_size, contrib_rows, 1, block_size)
    return (panels, top_update)


def solution(mesh):
    return jax.shard_map(
        shards,
        mesh=mesh,
        in_specs=(
            P("leaf", None, "row", None, None, "col", None),
            P("leaf", None, None),
            P(None, "leaf", None, "row", None, "col", None),
            P(None, "leaf", None, "row", None),
            P(),
            P(),
        ),
        out_specs=(
            P(None, "leaf", None, "row", None, "col", None),
            P("leaf", None, "row", None, None, "col", None),
        ),
        check_vma=False,
    )
```

profile of v0, /device:TPU:0, one launch (start us, length us, event | category | flops | bytes accessed | tf_op | source)
XLA Modules:
  0.0 749.0 jit_solution(1528554262989840019)
XLA Ops:
  9.0 11.4 %reduce.20 = f32[7,128,7,128]{3,2,1,0:T(8,128)} reduce(f32[1,7,1,128,7,1,128]{6,5,4,3,2,1,0:T(1,128)} %param.13, f32[]{:T(128)} %constant.368), dimensions={0,2,5}, to_apply=%param.13.reduce_sub_computation | reduce | bytes 6422532 | tf_op args[0]
  30.4 35.8 %all-gather.11.cloned.1.call-done = f32[2048,128]{1,0:T(8,128)} async-done(((f32[128,128]{1,0:T(8,128)}), f32[2048,128]{1,0:T(8,128)}) %all-gather.11.cloned.1.call-update) | async-done | bytes 1048592 | tf_op jit(solution)/shard_map/all_gather | solution.py:40
  71.4 11.7 %cholesky.286 = f32[128,128]{1,0:T(8,128)S(1)} custom-call(f32[128,128]{1,0:T(8,128)S(1)} %copy.125), custom_call_target="Cholesky" | custom-call | tf_op jit(solution)/shard_map/jit(cholesky)/cholesky | solution.py:49
  83.2 9.8 %custom-call.27 = f32[1,128,128]{1,2,0:T(8,128)S(1)} custom-call(f32[1,128,128]{2,1,0:T(8,128)S(1)} %get-tuple-element.106), custom_call_target="InvertDiagBlocksLowerTriangular" | custom-call | tf_op jit(solution)/shard_map/jit(cholesky)/cholesky | solution.py:49
  94.1 12.1 %cholesky.305 = f32[128,128]{1,0:T(8,128)S(1)} custom-call(f32[128,128]{1,0:T(8,128)S(1)} %copy.127), custom_call_target="Cholesky" | custom-call | tf_op jit(solution)/shard_map/jit(cholesky)/cholesky | solution.py:49
  106.2 9.8 %custom-call.28 = f32[1,128,128]{1,2,0:T(8,128)S(1)} custom-call(f32[1,128,128]{2,1,0:T(8,128)S(1)} %get-tuple-element.103), custom_call_target="InvertDiagBlocksLowerTriangular" | custom-call | tf_op jit(solution)/shard_map/jit(cholesky)/cholesky | solution.py:49
  117.0 11.7 %cholesky.326 = f32[128,128]{1,0:T(8,128)S(1)} custom-call(f32[128,128]{1,0:T(8,128)S(1)} %copy.129), custom_call_target="Cholesky" | custom-call | tf_op jit(solution)/shard_map/jit(cholesky)/cholesky | solution.py:49
  128.7 9.8 %custom-call.29 = f32[1,128,128]{1,2,0:T(8,128)S(1)} custom-call(f32[1,128,128]{2,1,0:T(8,128)S(1)} %get-tuple-element.100), custom_call_target="InvertDiagBlocksLowerTriangular" | custom-call | tf_op jit(solution)/shard_map/jit(cholesky)/cholesky | solution.py:49
  139.3 11.9 %cholesky.343 = f32[128,128]{1,0:T(8,128)S(1)} custom-call(f32[128,128]{1,0:T(8,128)S(1)} %copy.131), custom_call_target="Cholesky" | custom-call | tf_op jit(solution)/shard_map/jit(cholesky)/cholesky | solution.py:49
  165.1 39.3 %custom-call.30 = f32[4,128,128]{1,2,0:T(8,128)S(1)} custom-call(f32[4,128,128]{2,1,0:T(8,128)S(1)} %get-tuple-element.31), custom_call_target="InvertDiagBlocksLowerTriangular" | custom-call | tf_op jit(solution)/shard_map/triangular_solve/custom-call.3 | solution.py:50
  223.5 41.4 %all-reduce.4.cloned.1.call-done = f32[7,128,512]{2,1,0:T(8,128)} async-done(((f32[7,128,512]{2,1,0:T(8,128)}), f32[7,128,512]{2,1,0:T(8,128)}) %all-reduce.4.cloned.1.call-update) | async-done | bytes 1835024 | tf_op jit(solution)/shard_map/psum | solution.py:12
  301.3 92.5 %all-to-all-done = f32[16,4,128,128]{3,2,1,0:T(8,128)} async-done(((f32[16,4,128,128]{3,2,1,0:T(8,128)}), f32[16,4,128,128]{3,2,1,0:T(8,128)}, u32[]{:S(2)}, u32[]{:S(2)}) %all-to-all-start) | async-done | bytes 4194336 | tf_op jit(solution)/shard_map/all_to_all | solution.py:145
  413.3 69.7 %collective-permute-done = f32[7,128,7,128]{3,1,0,2:T(8,128)S(1)} collective-permute-done((f32[7,128,7,128]{3,1,0,2:T(8,128)S(1)}, f32[7,128,7,128]{3,1,0,2:T(8,128)S(1)}, u32[]{:S(2)}, u32[]{:S(2)}) %collective-permute-start) | collective-permute-done | bytes 3211296 | tf_op jit(solution)/shard_map/ppermute | solution.py:22
  489.4 34.7 %all-gather.13.cloned.1.call-done = f32[2048,128]{1,0:T(8,128)} async-done(((f32[128,128]{1,0:T(8,128)}), f32[2048,128]{1,0:T(8,128)}) %all-gather.13.cloned.1.call-update) | async-done | bytes 1048592 | tf_op jit(solution)/shard_map/all_gather | solution.py:40
  529.2 11.7 %cholesky.358 = f32[128,128]{1,0:T(8,128)S(1)} custom-call(f32[128,128]{1,0:T(8,128)S(1)} %cholesky.439), custom_call_target="Cholesky" | custom-call | tf_op jit(solution)/shard_map/jit(cholesky)/cholesky | solution.py:49
  541.0 9.8 %custom-call.31 = f32[1,128,128]{1,2,0:T(8,128)S(1)} custom-call(f32[1,128,128]{2,1,0:T(8,128)S(1)} %get-tuple-element.96), custom_call_target="InvertDiagBlocksLowerTriangular" | custom-call | tf_op jit(solution)/shard_map/jit(cholesky)/cholesky | solution.py:49
  551.6 11.9 %cholesky.377 = f32[128,128]{1,0:T(8,128)S(1)} custom-call(f32[128,128]{1,0:T(8,128)S(1)} %cholesky.443), custom_call_target="Cholesky" | custom-call | tf_op jit(solution)/shard_map/jit(cholesky)/cholesky | solution.py:49
  563.5 9.8 %custom-call.32 = f32[1,128,128]{1,2,0:T(8,128)S(1)} custom-call(f32[1,128,128]{2,1,0:T(8,128)S(1)} %get-tuple-element.93), custom_call_target="InvertDiagBlocksLowerTriangular" | custom-call | tf_op jit(solution)/shard_map/jit(cholesky)/cholesky | solution.py:49
  574.0 11.7 %cholesky.398 = f32[128,128]{1,0:T(8,128)S(1)} custom-call(f32[128,128]{1,0:T(8,128)S(1)} %cholesky.448), custom_call_target="Cholesky" | custom-call | tf_op jit(solution)/shard_map/jit(cholesky)/cholesky | solution.py:49
  585.8 9.8 %custom-call.33 = f32[1,128,128]{1,2,0:T(8,128)S(1)} custom-call(f32[1,128,128]{2,1,0:T(8,128)S(1)} %get-tuple-element.90), custom_call_target="InvertDiagBlocksLowerTriangular" | custom-call | tf_op jit(solution)/shard_map/jit(cholesky)/cholesky | solution.py:49
  596.2 12.1 %cholesky.415 = f32[128,128]{1,0:T(8,128)S(1)} custom-call(f32[128,128]{1,0:T(8,128)S(1)} %convolution_subtract_fusion.10), custom_call_target="Cholesky" | custom-call | tf_op jit(solution)/shard_map/jit(cholesky)/cholesky | solution.py:49
  622.2 39.3 %custom-call.34 = f32[4,128,128]{1,2,0:T(8,128)S(1)} custom-call(f32[4,128,128]{2,1,0:T(8,128)S(1)} %get-tuple-element.32), custom_call_target="InvertDiagBlocksLowerTriangular" | custom-call | tf_op jit(solution)/shard_map/triangular_solve/custom-call.3 | solution.py:50
  679.0 42.6 %all-reduce.6.cloned.1.call-done = f32[7,128,512]{2,1,0:T(8,128)} async-done(((f32[7,128,512]{2,1,0:T(8,128)}), f32[7,128,512]{2,1,0:T(8,128)}) %all-reduce.6.cloned.1.call-update) | async-done | bytes 1835024 | tf_op jit(solution)/shard_map/psum | solution.py:12
  724.1 10.3 %slice_subtract_fusion = f32[768,768]{1,0:T(8,128)} fusion(f32[896,896]{1,0:T(8,128)} %bitcast.197, f32[768,512]{1,0:T(8,128)S(1)} %bitcast.204, f32[768,128]{0,1:T(8,128)S(1)} %fusion.59, f32[768,128]{0,1:T(8,128)S(1)} %fusion.60, f32[768,128]{0,1:T(8,128)S(1)} %fusion.61, f32[768,128]{0,1:T(8,128)S(1)} %bitcast.194), kind=kOutput, calls=%fused_computation.18 | convolution fusion | flops 3625648128 | bytes 7864320 | tf_op jit(solution)/shard_map/ik,jk->ij/dot_general | solution.py:60
  (287 shorter events, 172.9 us)
Async XLA Ops:
  7.2 19.8 %copy-start = (s32[1,2,24]{2,1,0:T(2,128)S(1)}, s32[1,2,24]{2,1,0:T(2,128)}, u32[]{:S(2)}) copy-start(s32[1,2,24]{2,1,0:T(2,128)} %param.18) | copy-start | bytes 580
  7.2 59.1 %all-gather.11.cloned.1.call-start = ((), (), s32[]{:S(2)}) async-start(), calls=%async_computation.5 | async-start | bytes 1114112 | tf_op jit(solution)/shard_map/all_gather | solution.py:40
  8.9 11.5 %copy-start.14 = (f32[7,4,7,4]{3,2,1,0:T(8,128)}, f32[7,4,7,4]{3,2,1,0:T(8,128)S(1)}, u32[]{:S(2)}) copy-start(f32[7,4,7,4]{3,2,1,0:T(8,128)S(1)} %convert_element_type.75) | copy-start | bytes 9412
  24.8 44.0 %copy-start.3 = (f32[896,896]{1,0:T(8,128)}, f32[896,896]{1,0:T(8,128)S(1)}, u32[]{:S(2)}) copy-start(f32[896,896]{1,0:T(8,128)S(1)} %bitcast_multiply_fusion) | copy-start | bytes 9633796
  25.5 178.9 %all-gather.7.cloned.1.call-start = ((), (), s32[]{:S(2)}) async-start(), calls=%async_computation.1 | async-start | bytes 2293760 | tf_op jit(solution)/shard_map/all_gather | solution.py:48
  26.6 238.2 %all-reduce.4.cloned.1.call-start = ((), (), s32[]{:S(2)}) async-start(), calls=%async_computation.2 | async-start | bytes 3670016 | tf_op jit(solution)/shard_map/psum | solution.py:12
  26.9 43.6 %copy-start.16 = (s32[512]{0:T(512)}, s32[512]{0:T(512)S(1)}, u32[]{:S(2)}) copy-start(s32[512]{0:T(512)S(1)} %iota_add_fusion.2) | copy-start | bytes 6148
  29.9 40.3 %copy-start.21 = (s32[4,2]{0,1:T(2,128)}, s32[4,2]{0,1:T(2,128)S(1)}, u32[]{:S(2)}) copy-start(s32[4,2]{0,1:T(2,128)S(1)} %get-tuple-element.54) | copy-start | bytes 100
  210.7 4.2 copy-start.11
  219.7 47.5 %copy-start.26 = (pred[6]{0:T(512)(128)(4,1)}, pred[6]{0:T(512)(128)(4,1)S(1)}, u32[]{:S(2)}) copy-start(pred[6]{0:T(512)(128)(4,1)S(1)} %slice.251) | copy-start | bytes 22
  286.6 2.9 copy-start.18
  286.6 2.9 copy-start.29
  294.5 5.1 copy-start.19
  294.5 5.3 copy-start.25
  294.5 5.3 copy-start.15
  294.5 99.3 %all-to-all-start = ((f32[16,4,128,128]{3,2,1,0:T(8,128)}), f32[16,4,128,128]{3,2,1,0:T(8,128)}, u32[]{:S(2)}, u32[]{:S(2)}) async-start(f32[16,4,128,128]{3,2,1,0:T(8,128)} %bitcast.181), calls=%async_computation | async-start | bytes 8388608 | tf_op jit(solution)/shard_map/all_to_all | solution.py:145
  299.5 224.6 %all-gather.13.cloned.1.call-start = ((), (), s32[]{:S(2)}) async-start(), calls=%async_computation.6 | async-start | bytes 1114112 | tf_op jit(solution)/shard_map/all_gather | solution.py:40
  411.8 71.3 %collective-permute-start = (f32[7,128,7,128]{3,1,0,2:T(8,128)S(1)}, f32[7,128,7,128]{3,1,0,2:T(8,128)S(1)}, u32[]{:S(2)}, u32[]{:S(2)}) collective-permute-start(f32[7,128,7,128]{3,1,0,2:T(8,128)S(1)} %fusion.38), channel_id=1, source_target_pairs={{0,16},{16,0},{1,17},{17,1},{2,18},{18,2},{3,19},{19,3},{4,20},{20... | collective-permute-start | bytes 9633800 | tf_op jit(solution)/shard_map/ppermute | solution.py:22
  486.4 39.6 %copy-start.4 = (f32[112,8,7,128]{3,1,2,0:T(8,128)}, f32[112,8,7,128]{3,1,2,0:T(8,128)S(1)}, u32[]{:S(2)}) copy-start(f32[112,8,7,128]{3,1,2,0:T(8,128)S(1)} %copy.188) | copy-start | bytes 9633796
  487.1 174.4 %all-gather.9.cloned.1.call-start = ((), (), s32[]{:S(2)}) async-start(), calls=%async_computation.3 | async-start | bytes 2293760 | tf_op jit(solution)/shard_map/all_gather | solution.py:48
  489.2 232.4 %all-reduce.6.cloned.1.call-start = ((), (), s32[]{:S(2)}) async-start(), calls=%async_computation.4 | async-start | bytes 3670016 | tf_op jit(solution)/shard_map/psum | solution.py:12
  667.8 4.2 copy-start.10
  679.0 44.9 %copy-start.27 = (pred[6]{0:T(512)(128)(4,1)S(1)}, pred[6]{0:T(512)(128)(4,1)}, u32[]{:S(2)}) copy-start(pred[6]{0:T(512)(128)(4,1)} %copy-done.26) | copy-start | bytes 22
  736.9 5.0 copy-start.1
  (16 other events, 23.4 us)
Sparse Core Ops, SparseCore 0:
  25.6 40.5 all-gather.10
  68.4 40.9 all-gather.6
  218.7 46.0 all-reduce.3
  487.2 36.8 all-gather.12
  526.1 40.9 all-gather.8
  675.4 46.0 all-reduce.5
where the time goes:
time: 758 us; the launch traced here: 749 us
  waiting for transfers between devices  317 us (42%)
  other arithmetic  279 us (37%)
  local copies, waits for them, and re-layouts  81.2 us (11%)
  matrix products  44.7 us (6%)
  between operations  20.4 us (3%)
    another operation x31, other arithmetic, factor_whole(): pivot_factor = jnp.linalg.cholesky(symmetric_lower(corner))  159 us
    all_to_all x1, waiting for transfers between devices, shards(): lax.all_to_all(packed, ('row', 'col'), split_axis=0, concat_axis=0, tiled...  92.5 us
    psum x2, waiting for transfers between devices, from_root(): return lax.psum(kept, axis)  83.9 us
    another operation x5, other arithmetic, factor_whole(): lax.linalg.triangular_solve(pivot_factor, pivot_wide[block_size:], left_s...  79.2 us
    all_gather x2, waiting for transfers between devices, factor_whole(): lax.all_gather(front_local[None, :block_size, :block_size], ('row', 'col'...  70.5 us
    ppermute x1, waiting for transfers between devices, partner_2(): return lax.ppermute(block, axis, route)  69.7 us
    another operation x14, matrix products, factor_whole(): lax.linalg.triangular_solve(pivot_factor, pivot_wide[block_size:], left_s...  20.7 us
    dot_general x2, matrix products, factor_whole(): jnp.einsum('ik,jk->ij', rows_here[block_size:], picked_rows[block_size:],...  19.8 us
  transfers between devices with their start and end apart: 8, of which 6 were waited for; matrix products, arithmetic and copies ran while one was open for 38% of the time, Pallas kernels for 0%

commit v1 on v0

--- a/solution.py
+++ b/solution.py
@@ -1,6 +1,9 @@
+import functools
 import jax
 import jax.numpy as jnp
 from jax import lax
+from jax.experimental import pallas as pl
+from jax.experimental.pallas import tpu as pltpu
 from jax.sharding import PartitionSpec as P
 
 highest = lax.Precision.HIGHEST
@@ -33,6 +36,118 @@
     return picked[:, None, :, None]
 
 
+def eliminate_block(block):
+    size = block.shape[0]
+    groups = size // 8
+    lane = lax.broadcasted_iota(jnp.int32, (8, size), 1)
+    sub = lax.broadcasted_iota(jnp.int32, (8, size), 0)
+    rows = [block[8 * g : 8 * g + 8, :] for g in range(groups)]
+    for g in range(groups):
+        base = 8 * g
+        here = rows[g]
+        inside = jnp.logical_and(lane >= base, lane < base + 8)
+        line = [jnp.broadcast_to(here[a : a + 1, :], (8, size)) for a in range(8)]
+        s = [
+            [
+                jnp.broadcast_to(line[a][:, base + b : base + b + 1], (8, size)) if b >= a else None
+                for b in range(8)
+            ]
+            for a in range(8)
+        ]
+        line = [
+            jnp.where(inside, jnp.where(lane == base + a, 1.0, 0.0), line[a]) for a in range(8)
+        ]
+        inverse = [None] * 8
+        ratio = [[None] * 8 for _ in range(8)]
+        for a in range(8):
+            inverse[a] = 1.0 / s[a][a]
+            for b in range(a + 1, 8):
+                ratio[a][b] = s[a][b] * inverse[a]
+            for b in range(a + 1, 8):
+                for c in range(b, 8):
+                    s[b][c] = s[b][c] - ratio[a][b] * s[a][c]
+                line[b] = line[b] - ratio[a][b] * line[a]
+        done = line[0]
+        for a in range(8):
+            whole = line[a]
+            for b in range(a, 8):
+                whole = jnp.where(lane == base + b, s[a][b], whole)
+            done = whole if a == 0 else jnp.where(sub == a, whole, done)
+        rows[g] = done
+        if g + 1 < groups:
+            solved = [None] * 8
+            for a in range(7, -1, -1):
+                total = line[a] * inverse[a]
+                for b in range(a + 1, 8):
+                    total = total - ratio[a][b] * solved[b]
+                solved[a] = total
+            for h in range(g + 1, groups):
+                before = rows[h]
+                total = jnp.where(inside, 0.0, before)
+                for a in range(8):
+                    spread = jnp.broadcast_to(before[:, base + a : base + a + 1], (8, size))
+                    total = total - spread * solved[a]
+                rows[h] = total
+    return jnp.concatenate(rows, axis=0)
+
+
+def pivot_kernel(block_size, corner_ref, upper_ref, inverse_ref, row_ref):
+    order = corner_ref.shape[0]
+    inverse_ref[...] = corner_ref[...]
+    row_id = lax.broadcasted_iota(jnp.int32, (block_size, block_size), 0)
+    col_id = lax.broadcasted_iota(jnp.int32, (block_size, block_size), 1)
+    wide_col = lax.broadcasted_iota(jnp.int32, (block_size, order), 1)
+    tall_row = lax.broadcasted_iota(jnp.int32, (order, block_size), 0)
+
+    def step(k, carry):
+        start = pl.multiple_of(k * block_size, block_size)
+        here = pl.ds(start, block_size)
+        reduced = eliminate_block(inverse_ref[here, here])
+        pivot = jnp.sum(jnp.where(row_id == col_id, reduced, 0.0), axis=1, keepdims=True)
+        scale = lax.rsqrt(pivot)
+        scale = scale * (1.5 - 0.5 * pivot * scale * scale)
+        scaled = reduced * scale
+        small = jnp.where(row_id > col_id, scaled, jnp.where(row_id == col_id, scale, 0.0))
+        row = jnp.dot(
+            small, inverse_ref[here, :], precision=highest, preferred_element_type=jnp.float32
+        )
+        right = jnp.where(wide_col >= start + block_size, row, 0.0)
+        upper_ref[here, :] = right
+        upper_ref[here, here] = jnp.where(row_id <= col_id, scaled, 0.0)
+        row_ref[...] = row
+        row_ref[:, here] = small
+        inverse_ref[:, here] = jnp.where(
+            tall_row >= start + block_size, 0.0, inverse_ref[:, here]
+        )
+        inverse_ref[...] = inverse_ref[...] - lax.dot_general(
+            right,
+            row_ref[...],
+            (((0,), (0,)), ((), ())),
+            precision=highest,
+            preferred_element_type=jnp.float32,
+        )
+        inverse_ref[here, :] = jnp.where(wide_col < start + block_size, row_ref[...], 0.0)
+        return carry
+
+    lax.fori_loop(0, order // block_size, step, 0)
+
+
+def pivot_factors(corner, block_size):
+    order = corner.shape[0]
+    shape = jax.ShapeDtypeStruct((order, order), jnp.float32)
+    return pl.pallas_call(
+        functools.partial(pivot_kernel, block_size),
+        out_shape=(shape, shape),
+        in_specs=[pl.BlockSpec(memory_space=pltpu.VMEM)],
+        out_specs=(pl.BlockSpec(memory_space=pltpu.VMEM),) * 2,
+        scratch_shapes=[pltpu.VMEM((block_size, order), jnp.float32)],
+        cost_estimate=pl.CostEstimate(
+            flops=64 * order**3, bytes_accessed=64 * 4 * order * order, transcendentals=0
+        ),
+        name="pivot_factors",
+    )(corner)
+
+
 def factor_whole(front_local, my_row, my_col, grid_side, block_size, kept):
     local_order = front_local.shape[0]
     block_rows = local_order // block_size
@@ -46,11 +161,15 @@
         .reshape(pivots, pivots)
     )
     pivot_wide = lax.all_gather(front_local[:, :block_size], "col", axis=1, tiled=True)
-    pivot_factor = jnp.linalg.cholesky(symmetric_lower(corner))
-    solved = lax.linalg.triangular_solve(
-        pivot_factor, pivot_wide[block_size:], left_side=False, lower=True, transpose_a=True
-    )
-    top_rows = lax.dynamic_slice(pivot_factor, (my_row * block_size, 0), (block_size, pivots))
+    upper, inverse = pivot_factors(symmetric_lower(corner), block_size)
+    solved = jnp.einsum(
+        "ik,jk->ij",
+        pivot_wide[block_size:],
+        inverse,
+        precision=highest,
+        preferred_element_type=jnp.float32,
+    )
+    top_rows = lax.dynamic_slice(upper, (0, my_row * block_size), (pivots, block_size)).T
     rows_here = jnp.concatenate([top_rows, solved], axis=0)
     rows_there = from_root(rows_here, "row", my_col)
     picked_rows = jnp.take(
@@ -61,7 +180,7 @@
         "ik,jk->ij",
         rows_here[block_size:],
         picked_rows[block_size:],
-        precision=highest,
+        precision=lax.Precision.HIGH,
         preferred_element_type=jnp.float32,
     )
     return (panel_col, update)
@@ -69,6 +188,28 @@
 
 def factor(front_local, my_row, my_col, grid_side, block_size, kept):
     return factor_whole(front_local, my_row, my_col, grid_side, block_size, kept)
+
+
+def pack_lower(front):
+    return jnp.concatenate(
+        [front[t, :, : t + 1, :].reshape(front.shape[1], -1) for t in range(front.shape[0])],
+        axis=1,
+    )
+
+
+def unpack_lower(packed, block_rows):
+    block_size = packed.shape[0]
+    rows = []
+    start = 0
+    for t in range(block_rows):
+        width = (t + 1) * block_size
+        rows.append(
+            jnp.pad(
+                packed[:, start : start + width], ((0, 0), (0, block_rows * block_size - width))
+            )
+        )
+        start += width
+    return jnp.concatenate(rows, axis=0)
 
 
 def route_tables(child_map, grid_side, my_index, block_rows):
@@ -162,7 +303,9 @@
         own_front = own_front.at[:, :, 0, :].add(mask_here[:, :, 0, :] * acc_panel[depth])
         if depth + 1 < levels:
             partner, partner_panel, partner_diag = partner_2(
-                (own_front, acc_panel[depth + 1 :], acc_diag[depth + 1 :]), "leaf", depth
+                (pack_lower(own_front), acc_panel[depth + 1 :], acc_diag[depth + 1 :]),
+                "leaf",
+                depth,
             )
             acc_panel = jnp.concatenate(
                 [acc_panel[: depth + 1], acc_panel[depth + 1 :] + partner_panel], axis=0
@@ -171,8 +314,10 @@
                 [acc_diag[: depth + 1], acc_diag[depth + 1 :] + partner_diag], axis=0
             )
         else:
-            partner = partner_2(own_front, "leaf", depth)
-        front_local = (own_front + partner).reshape(local_order, local_order)
+            partner = partner_2(pack_lower(own_front), "leaf", depth)
+        front_local = own_front.reshape(local_order, local_order) + unpack_lower(
+            partner, block_rows
+        )
         panel_col, update = factor(front_local, my_row, my_col, grid_side, block_size, all_blocks)
         panel_list.append(panel_col)
     panels = jnp.stack(panel_list).reshape(levels + 1, 1, block_rows, 1, block_size, 1, block_size)

time: 758 us -> 545 us (0.72)
  other arithmetic: 279 us -> 51 us
  Pallas kernels: 0 us -> 66.1 us
  matrix products: 44.7 us -> 19.1 us
  waiting for transfers between devices: 317 us -> 292 us
    another operation x36 -> x0, other arithmetic: 238 us -> none  [the longest x31 159 us: factor_whole(): pivot_factor = jnp.linalg.cholesky(symmetric_lower(corner))]
    pallas_call x0 -> x2, Pallas kernels: none -> 66.1 us  [pivot_factors(): pl.pallas_call(functools.partial(pivot_kernel, block_size), out_shape=(sh...]
    ppermute x1, waiting for transfers between devices: 69.7 us -> 38.6 us  [partner_2(): return lax.ppermute(block, axis, route)]
    another operation x26 -> x0, matrix products: 25 us -> none  [the longest x14 20.7 us: factor_whole(): lax.linalg.triangular_solve(pivot_factor, pivot_wide[block_size:], left_s...]
    another operation x39 -> x4, local copies, waits for them, and re-layouts: 15.7 us -> 2.08 us  [pack_lower(): front[t, :, :t + 1, :].reshape(front.shape[1], -1)]
    dot_general x2, matrix products: 19.8 us -> 10.3 us  [factor_whole(): jnp.einsum('ik,jk->ij', rows_here[block_size:], picked_rows[block_size:],...]
    dot_general x0 -> x2, matrix products: none -> 8.73 us  [factor_whole(): jnp.einsum('ik,jk->ij', pivot_wide[block_size:], inverse, precision=highe...]
    unnamed x68 -> x54, local copies, waits for them, and re-layouts: 11.1 us -> 17.5 us
  transfers between devices with their start and end apart: 8 -> 8, of which waited for: 6 -> 8; matrix products, arithmetic and copies ran while one was open for 38% -> 6% of each run, Pallas kernels for 0% -> 12%
where the time goes in v1:
time: 545 us; the launch traced here: 534 us
  waiting for transfers between devices  292 us (54%)
  local copies, waits for them, and re-layouts  84.7 us (16%)
  Pallas kernels  66.1 us (12%)
  other arithmetic  51 us (9%)
  matrix products  19.1 us (4%)
  between operations  15.2 us (3%)
  starting transfers between devices  6.67 us (1%)
    all_to_all x1, waiting for transfers between devices, shards(): lax.all_to_all(packed, ('row', 'col'), split_axis=0, concat_axis=0, tiled...  93.4 us
    psum x2, waiting for transfers between devices, from_root(): return lax.psum(kept, axis)  84.6 us
    all_gather x2, waiting for transfers between devices, factor_whole(): lax.all_gather(front_local[None, :block_size, :block_size], ('row', 'col'...  71.5 us
    pallas_call x2, Pallas kernels, pivot_factors(): pl.pallas_call(functools.partial(pivot_kernel, block_size), out_shape=(sh...  66.1 us
    ppermute x1, waiting for transfers between devices, partner_2(): return lax.ppermute(block, axis, route)  38.6 us
    unnamed x54, local copies, waits for them, and re-layouts  17.5 us
    unnamed x2, other arithmetic  11.4 us
    reshape x3, local copies, waits for them, and re-layouts, shards(): update.reshape(contrib_rows, block_size, contrib_rows, block_size)  11.4 us
  transfers between devices with their start and end apart: 8, of which 8 were waited for; matrix products, arithmetic and copies ran while one was open for 6% of the time, Pallas kernels for 12%

profile of v1, /device:TPU:0, one launch (start us, length us, event | category | flops | bytes accessed | tf_op | source)
XLA Modules:
  0.0 534.3 jit_solution(496260170684013354)
XLA Ops:
  9.0 11.4 %reduce.4 = f32[7,128,7,128]{3,2,1,0:T(8,128)} reduce(f32[1,7,1,128,7,1,128]{6,5,4,3,2,1,0:T(1,128)} %param.10, f32[]{:T(128)} %constant.257), dimensions={0,2,5}, to_apply=%param.10.reduce_sub_computation | reduce | bytes 6422532 | tf_op args[0]
  30.0 37.0 %all-gather.11.cloned.1.call-done = f32[2048,128]{1,0:T(8,128)} async-done(((f32[128,128]{1,0:T(8,128)}), f32[2048,128]{1,0:T(8,128)}) %all-gather.11.cloned.1.call-update) | async-done | bytes 1048592 | tf_op jit(solution)/shard_map/all_gather | solution.py:155
  73.1 33.2 %pivot_factors.2 = (f32[512,512]{1,0:T(8,128)}, f32[512,512]{1,0:T(8,128)}) custom-call(f32[512,512]{1,0:T(8,128)} %copy.111.corner_ref), custom_call_target="tpu_custom_call" | custom-call | flops 8589934592 | bytes 67108864 | tf_op jit(solution)/shard_map/pivot_factors/pallas_call | solution.py:138
  110.2 4.3 fusion.5
  119.7 41.7 %all-reduce.8.cloned.1.call-done = f32[7,128,512]{2,1,0:T(8,128)} async-done(((f32[7,128,512]{2,1,0:T(8,128)}), f32[7,128,512]{2,1,0:T(8,128)}) %all-reduce.8.cloned.1.call-update) | async-done | bytes 1835024 | tf_op jit(solution)/shard_map/psum | solution.py:15
  164.4 5.2 slice_subtract_fusion.1
  169.6 3.9 reshape.664
  177.3 4.2 gather_fusion
  181.5 4.1 select_multiply_fusion
  185.6 4.6 gather_fusion.1
  190.3 5.0 fusion
  195.3 5.0 all-to-all-start
  201.1 93.4 %all-to-all-done = f32[16,4,128,128]{3,2,1,0:T(8,128)} async-done(((f32[16,4,128,128]{3,2,1,0:T(8,128)}), f32[16,4,128,128]{3,2,1,0:T(8,128)}, u32[]{:S(2)}, u32[]{:S(2)}) %all-to-all-start) | async-done | bytes 4194336 | tf_op jit(solution)/shard_map/all_to_all | solution.py:286
  294.5 4.7 copy.122
  299.2 4.8 gather_fusion.2
  304.0 4.4 broadcast_select_fusion
  308.4 4.5 gather_fusion.3
  331.8 38.6 %collective-permute-done = f32[128,3584]{1,0:T(8,128)S(1)} collective-permute-done((f32[128,3584]{1,0:T(8,128)}, f32[128,3584]{1,0:T(8,128)S(1)}, u32[]{:S(2)}, u32[]{:S(2)}) %collective-permute-start) | collective-permute-done | bytes 1835040 | tf_op jit(solution)/shard_map/ppermute | solution.py:25
  376.6 34.4 %all-gather.13.cloned.1.call-done = f32[2048,128]{1,0:T(8,128)} async-done(((f32[128,128]{1,0:T(8,128)}), f32[2048,128]{1,0:T(8,128)}) %all-gather.13.cloned.1.call-update) | async-done | bytes 1048592 | tf_op jit(solution)/shard_map/all_gather | solution.py:155
  418.8 33.0 %pivot_factors.3 = (f32[512,512]{1,0:T(8,128)}, f32[512,512]{1,0:T(8,128)}) custom-call(f32[512,512]{1,0:T(8,128)} %fusion.8.corner_ref), custom_call_target="tpu_custom_call" | custom-call | flops 8589934592 | bytes 67108864 | tf_op jit(solution)/shard_map/pivot_factors/pallas_call | solution.py:138
  454.0 4.4 fusion.3
  462.8 42.9 %all-reduce.10.cloned.1.call-done = f32[7,128,512]{2,1,0:T(8,128)} async-done(((f32[7,128,512]{2,1,0:T(8,128)}), f32[7,128,512]{2,1,0:T(8,128)}) %all-reduce.10.cloned.1.call-update) | async-done | bytes 1835024 | tf_op jit(solution)/shard_map/psum | solution.py:15
  510.8 5.2 slice_subtract_fusion
  523.2 3.8 copy.139
  (190 shorter events, 85.4 us)
Async XLA Ops:
  7.2 21.1 %copy-start = (s32[1,2,24]{2,1,0:T(2,128)S(1)}, s32[1,2,24]{2,1,0:T(2,128)}, u32[]{:S(2)}) copy-start(s32[1,2,24]{2,1,0:T(2,128)} %param.15) | copy-start | bytes 580
  7.2 59.9 %all-gather.11.cloned.1.call-start = ((), (), s32[]{:S(2)}) async-start(), calls=%async_computation.5 | async-start | bytes 1114112 | tf_op jit(solution)/shard_map/all_gather | solution.py:155
  20.4 2.0 copy-start.4
  24.0 1.7 copy-start.6
  26.3 83.9 %all-gather.7.cloned.1.call-start = ((), (), s32[]{:S(2)}) async-start(), calls=%async_computation.1 | async-start | bytes 2293760 | tf_op jit(solution)/shard_map/all_gather | solution.py:163
  28.2 133.2 %all-reduce.8.cloned.1.call-start = ((), (), s32[]{:S(2)}) async-start(), calls=%async_computation.2 | async-start | bytes 3670016 | tf_op jit(solution)/shard_map/psum | solution.py:15
  107.3 8.6 %copy-start.7 = (f32[128,512]{1,0:T(8,128)}, f32[128,512]{1,0:T(8,128)S(1)}, u32[]{:S(2)}) copy-start(f32[128,512]{1,0:T(8,128)S(1)} %copy.112) | copy-start | bytes 786436
  177.3 4.2 copy-start.16
  177.3 4.2 copy-start.19
  185.6 4.6 copy-start.18
  195.3 5.1 copy-start.13
  195.3 5.3 copy-start.14
  195.3 99.3 %all-to-all-start = ((f32[16,4,128,128]{3,2,1,0:T(8,128)}), f32[16,4,128,128]{3,2,1,0:T(8,128)}, u32[]{:S(2)}, u32[]{:S(2)}) async-start(f32[16,4,128,128]{3,2,1,0:T(8,128)} %bitcast.104), calls=%async_computation | async-start | bytes 8388608 | tf_op jit(solution)/shard_map/all_to_all | solution.py:286
  200.2 210.8 %all-gather.13.cloned.1.call-start = ((), (), s32[]{:S(2)}) async-start(), calls=%async_computation.6 | async-start | bytes 1114112 | tf_op jit(solution)/shard_map/all_gather | solution.py:155
  312.9 3.0 copy-start.12
  321.6 4.5 copy-start.11
  322.0 7.9 %copy-start.3 = (f32[7,128,7,128]{3,1,2,0:T(8,128)S(1)}, f32[7,128,7,128]{3,1,2,0:T(8,128)}, u32[]{:S(2)}) copy-start(f32[7,128,7,128]{3,1,2,0:T(8,128)} %copy-done.2) | copy-start | bytes 9633796
  328.4 41.9 %copy-start.17 = (pred[896]{0:T(1024)(128)(4,1)S(1)}, pred[896]{0:T(1024)(128)(4,1)}, u32[]{:S(2)}) copy-start(pred[896]{0:T(1024)(128)(4,1)} %constant.238.clone.1) | copy-start | bytes 2692
  328.4 41.9 %collective-permute-start = (f32[128,3584]{1,0:T(8,128)}, f32[128,3584]{1,0:T(8,128)S(1)}, u32[]{:S(2)}, u32[]{:S(2)}) collective-permute-start(f32[128,3584]{1,0:T(8,128)} %constant_dynamic-update-slice_fusion), channel_id=1, source_target_pairs={{0,16},{16,0},{1,17},{17,1},{2,18},{18,2},{3,19},{19,3},{4,20},{20... | collective-permute-start | bytes 5505032 | tf_op jit(solution)/shard_map/ppermute | solution.py:25
  374.0 80.0 %all-gather.9.cloned.1.call-start = ((), (), s32[]{:S(2)}) async-start(), calls=%async_computation.3 | async-start | bytes 2293760 | tf_op jit(solution)/shard_map/all_gather | solution.py:163
  375.9 129.8 %all-reduce.10.cloned.1.call-start = ((), (), s32[]{:S(2)}) async-start(), calls=%async_computation.4 | async-start | bytes 3670016 | tf_op jit(solution)/shard_map/psum | solution.py:15
  454.0 4.4 copy-start.9
  460.9 48.2 %copy-start.15 = (pred[6]{0:T(512)(128)(4,1)S(1)}, pred[6]{0:T(512)(128)(4,1)}, u32[]{:S(2)}) copy-start(pred[6]{0:T(512)(128)(4,1)} %slice.154) | copy-start | bytes 22
  519.7 7.3 %copy-start.1 = (s32[1,2,24]{2,1,0:T(2,128)S(1)}, s32[1,2,24]{2,1,0:T(2,128)}, u32[]{:S(2)}) copy-start(s32[1,2,24]{2,1,0:T(2,128)} %param.15) | copy-start | bytes 580
  (4 other events, 5.9 us)
Sparse Core Ops, SparseCore 0:
  26.4 40.5 all-gather.10
  69.2 40.9 all-gather.6
  116.1 45.2 all-reduce.7
  374.2 36.8 all-gather.12
  413.0 40.9 all-gather.8
  460.0 45.6 all-reduce.9

commit v2 on v1

--- a/solution.py
+++ b/solution.py
@@ -148,46 +148,109 @@
     )(corner)
 
 
-def factor_whole(front_local, my_row, my_col, grid_side, block_size, kept):
-    local_order = front_local.shape[0]
-    block_rows = local_order // block_size
+def rows_times(left, right, precision=highest):
+    return jnp.einsum(
+        "ik,jk->ij", left, right, precision=precision, preferred_element_type=jnp.float32
+    )
+
+
+def gather_corner(front_local, grid_side, block_size):
     pivots = grid_side * block_size
     squares = lax.all_gather(
         front_local[None, :block_size, :block_size], ("row", "col"), axis=0, tiled=True
     )
-    corner = (
+    return (
         squares.reshape(grid_side, grid_side, block_size, block_size)
         .transpose(0, 2, 1, 3)
         .reshape(pivots, pivots)
     )
-    pivot_wide = lax.all_gather(front_local[:, :block_size], "col", axis=1, tiled=True)
+
+
+def top_block(upper, my_row, my_col, block_size):
+    start = (my_col * block_size, my_row * block_size)
+    block = lax.dynamic_slice(upper, (start[1], start[0]), (block_size, block_size))
+    flipped = lax.dynamic_slice(upper, start, (block_size, block_size)).T
+    return jnp.where(my_row >= my_col, flipped, jnp.zeros_like(block))
+
+
+def factor_top(front_local, my_row, my_col, grid_side, block_size):
+    corner = gather_corner(front_local, grid_side, block_size)
+    wide = lax.all_gather(front_local[block_size:, :block_size], "col", axis=1, tiled=True)
     upper, inverse = pivot_factors(symmetric_lower(corner), block_size)
-    solved = jnp.einsum(
-        "ik,jk->ij",
-        pivot_wide[block_size:],
-        inverse,
-        precision=highest,
-        preferred_element_type=jnp.float32,
-    )
-    top_rows = lax.dynamic_slice(upper, (0, my_row * block_size), (pivots, block_size)).T
-    rows_here = jnp.concatenate([top_rows, solved], axis=0)
+    rows_here = rows_times(wide, inverse)
     rows_there = from_root(rows_here, "row", my_col)
-    picked_rows = jnp.take(
-        rows_there.reshape(block_rows, block_size, pivots), kept, axis=0
-    ).reshape(-1, pivots)
-    panel_col = lax.dynamic_slice(rows_here, (0, my_col * block_size), (local_order, block_size))
-    update = front_local[block_size:, block_size:] - jnp.einsum(
-        "ik,jk->ij",
-        rows_here[block_size:],
-        picked_rows[block_size:],
-        precision=lax.Precision.HIGH,
-        preferred_element_type=jnp.float32,
+    own = lax.dynamic_slice(
+        rows_here, (0, my_col * block_size), (rows_here.shape[0], block_size)
+    )
+    panel_col = jnp.concatenate([top_block(upper, my_row, my_col, block_size), own], axis=0)
+    update = front_local[block_size:, block_size:] - rows_times(
+        rows_here, rows_there, lax.Precision.HIGH
     )
     return (panel_col, update)
 
 
-def factor(front_local, my_row, my_col, grid_side, block_size, kept):
-    return factor_whole(front_local, my_row, my_col, grid_side, block_size, kept)
+def factor_child(front_local, my_row, my_col, grid_side, block_size, row_table, col_table):
+    local_order = front_local.shape[0]
+    block_rows = local_order // block_size
+    contrib_rows = block_rows - 1
+    row_src, row_ok, row_place, row_in = row_table
+    col_src, col_ok, col_place, col_in = col_table
+    corner = gather_corner(front_local, grid_side, block_size)
+    left = front_local[block_size:, :block_size].reshape(contrib_rows, block_size, block_size)
+    packed_left = jnp.take(left, row_src, axis=0) * row_ok[:, None, None]
+    received_left = lax.all_to_all(
+        packed_left.reshape(grid_side, slot_limit, block_size, block_size),
+        "row",
+        split_axis=0,
+        concat_axis=0,
+        tiled=True,
+    ).reshape(grid_side * slot_limit, block_size, block_size)
+    placed_left = jnp.take(received_left, row_place, axis=0) * row_in[:, None, None]
+    wide = lax.all_gather(
+        jnp.concatenate([left, placed_left], axis=0).reshape(-1, block_size),
+        "col",
+        axis=1,
+        tiled=True,
+    )
+    own_wide = wide[: contrib_rows * block_size]
+    placed_wide = wide[contrib_rows * block_size :]
+    there_wide = from_root(placed_wide, "row", my_col)
+    blocks = front_local[block_size:, block_size:].reshape(
+        contrib_rows, block_size, contrib_rows, block_size
+    )
+    packed = jnp.take(blocks.transpose(0, 2, 1, 3), row_src, axis=0)
+    packed = jnp.take(packed, col_src, axis=1)
+    packed = packed * (row_ok[:, None] * col_ok[None, :])[:, :, None, None]
+    packed = packed.reshape(
+        grid_side, slot_limit, grid_side, slot_limit, block_size, block_size
+    )
+    packed = packed.transpose(0, 2, 1, 3, 4, 5).reshape(
+        grid_side * grid_side, slot_limit * slot_limit, block_size, block_size
+    )
+    received = lax.all_to_all(packed, ("row", "col"), split_axis=0, concat_axis=0, tiled=True)
+    received = received.reshape(
+        grid_side, grid_side, slot_limit, slot_limit, block_size, block_size
+    )
+    received = received.transpose(0, 2, 1, 3, 4, 5).reshape(
+        grid_side * slot_limit, grid_side * slot_limit, block_size, block_size
+    )
+    placed = jnp.take(received, row_place, axis=0)
+    placed = jnp.take(placed, col_place, axis=1)
+    placed = placed * (row_in[:, None] * col_in[None, :])[:, :, None, None]
+    spread = placed.transpose(0, 2, 1, 3).reshape(local_order, local_order)
+    upper, inverse = pivot_factors(symmetric_lower(corner), block_size)
+    own_inverse = lax.dynamic_slice(
+        inverse, (my_col * block_size, 0), (block_size, inverse.shape[1])
+    )
+    panel_col = jnp.concatenate(
+        [top_block(upper, my_row, my_col, block_size), rows_times(own_wide, own_inverse)], axis=0
+    )
+    moved = spread - rows_times(
+        rows_times(placed_wide, inverse),
+        rows_times(there_wide, inverse),
+        lax.Precision.HIGH,
+    )
+    return (panel_col, moved.reshape(block_rows, block_size, block_rows, block_size))
 
 
 def pack_lower(front):
@@ -253,13 +316,11 @@
     my_row = lax.axis_index("row")
     my_col = lax.axis_index("col")
     my_leaf = lax.axis_index("leaf")
-    all_blocks = jnp.arange(block_rows, dtype=jnp.int32)
     leaf_local = leaf_front[0, :, 0, :, :, 0, :]
     front_local = (
         leaf_local * local_mask(leaf_pattern[0], my_row, my_col, block_rows, grid_side)
     ).reshape(local_order, local_order)
-    panel_col, update = factor(front_local, my_row, my_col, grid_side, block_size, all_blocks)
-    panel_list = [panel_col]
+    panel_list = []
     acc_panel = parent_panel.reshape(levels, block_rows, block_size, block_size)
     acc_diag = parent_diag.reshape(levels, block_rows, block_size)
     block_same = (
@@ -274,26 +335,16 @@
         child_map = lax.dynamic_index_in_dim(ext_map[depth], child_node, 0, keepdims=False)
         row_src, row_ok, row_place, row_in = route_tables(child_map, grid_side, my_row, block_rows)
         col_src, col_ok, col_place, col_in = route_tables(child_map, grid_side, my_col, block_rows)
-        update_blocks = update.reshape(contrib_rows, block_size, contrib_rows, block_size)
-        rows_taken = jnp.take(update_blocks, row_src, axis=0) * row_ok[:, None, None, None]
-        packed = jnp.take(rows_taken, col_src, axis=2) * col_ok[None, None, :, None]
-        packed = packed.reshape(
-            grid_side, slot_limit, block_size, grid_side, slot_limit, block_size
-        )
-        packed = packed.transpose(0, 3, 1, 4, 2, 5).reshape(
-            grid_side * grid_side, slot_limit * slot_limit, block_size, block_size
-        )
-        received = lax.all_to_all(packed, ("row", "col"), split_axis=0, concat_axis=0, tiled=True)
-        received = received.reshape(
-            grid_side, grid_side, slot_limit, slot_limit, block_size, block_size
-        )
-        received = received.transpose(0, 2, 1, 3, 4, 5).reshape(
-            grid_side * slot_limit, grid_side * slot_limit, block_size, block_size
-        )
-        placed = jnp.take(received, row_place, axis=0)
-        placed = jnp.take(placed, col_place, axis=1)
-        placed = placed * (row_in[:, None, None, None] * col_in[None, :, None, None])
-        spread = placed.transpose(0, 2, 1, 3)
+        panel_col, spread = factor_child(
+            front_local,
+            my_row,
+            my_col,
+            grid_side,
+            block_size,
+            (row_src, row_ok, row_place, row_in),
+            (col_src, col_ok, col_place, col_in),
+        )
+        panel_list.append(panel_col)
         parent_node = jnp.right_shift(my_leaf, depth + 1)
         pattern = lax.dynamic_index_in_dim(parent_pattern[depth], parent_node, 0, keepdims=False)
         mask_here = local_mask(pattern, my_row, my_col, block_rows, grid_side)
@@ -318,8 +369,8 @@
         front_local = own_front.reshape(local_order, local_order) + unpack_lower(
             partner, block_rows
         )
-        panel_col, update = factor(front_local, my_row, my_col, grid_side, block_size, all_blocks)
-        panel_list.append(panel_col)
+    panel_col, update = factor_top(front_local, my_row, my_col, grid_side, block_size)
+    panel_list.append(panel_col)
     panels = jnp.stack(panel_list).reshape(levels + 1, 1, block_rows, 1, block_size, 1, block_size)
     element_ids = jnp.arange(block_size)
     row_ids = (grid_side * (jnp.arange(contrib_rows) + 1) + my_row)[

time: 545 us -> 513 us (0.941)
  waiting for transfers between devices: 292 us -> 242 us
  matrix products: 19.1 us -> 29.9 us
  starting transfers between devices: 6.67 us -> 14.5 us
    all_to_all x1 -> x2, waiting for transfers between devices: 93.4 us -> 0.01 us  [the longest x1 0.01 us: factor_child(): lax.all_to_all(packed, ('row', 'col'), split_axis=0, concat_axis=0, tiled...]
    all_gather x4, waiting for transfers between devices: 74.8 us -> 163 us  [the longest x1 129 us: factor_child(): lax.all_gather(jnp.concatenate([left, placed_left], axis=0).reshape(-1, b...]
    psum x2, waiting for transfers between devices: 84.6 us -> 40.9 us  [from_root(): return lax.psum(kept, axis)]
    dot_general x4 -> x6, matrix products: 19.1 us -> 29.9 us  [rows_times(): jnp.einsum('ik,jk->ij', left, right, precision=precision, preferred_eleme...]
    slice x12, local copies, waits for them, and re-layouts: 1.7 us -> 12.1 us  [pack_lower(): front[t, :, :t + 1, :].reshape(front.shape[1], -1)]
    reshape x3 -> x1, local copies, waits for them, and re-layouts: 11.4 us -> 2.5 us  [shards(): update.reshape(contrib_rows, block_size, contrib_rows, block_size)]
    all_to_all x1 -> x2, starting transfers between devices: 4.95 us -> 12.7 us  [the longest x1 7.96 us: factor_child(): lax.all_to_all(packed, ('row', 'col'), split_axis=0, concat_axis=0, tiled...]
    gather x6, local copies, waits for them, and re-layouts: 23.7 us -> 16.7 us  [the longest x1 4.76 us: factor_child(): placed = jnp.take(received, row_place, axis=0)]
  transfers between devices with their start and end apart: 8 -> 9, of which waited for: 8 -> 5; matrix products, arithmetic and copies ran while one was open for 6% -> 15% of each run, Pallas kernels for 12% -> 13%
where the time goes in v2:
time: 513 us; the launch traced here: 503 us
  waiting for transfers between devices  242 us (47%)
  local copies, waits for them, and re-layouts  85 us (17%)
  Pallas kernels  66 us (13%)
  other arithmetic  50.5 us (10%)
  matrix products  29.9 us (6%)
  between operations  15 us (3%)
  starting transfers between devices  14.5 us (3%)
    all_gather x1, waiting for transfers between devices, factor_child(): lax.all_gather(jnp.concatenate([left, placed_left], axis=0).reshape(-1, b...  129 us
    pallas_call x2, Pallas kernels, pivot_factors(): pl.pallas_call(functools.partial(pivot_kernel, block_size), out_shape=(sh...  66 us
    psum x2, waiting for transfers between devices, from_root(): return lax.psum(kept, axis)  40.9 us
    ppermute x1, waiting for transfers between devices, partner_2(): return lax.ppermute(block, axis, route)  38.2 us
    all_gather x2, waiting for transfers between devices, gather_corner(): lax.all_gather(front_local[None, :block_size, :block_size], ('row', 'col'...  33.4 us
    dot_general x6, matrix products, rows_times(): jnp.einsum('ik,jk->ij', left, right, precision=precision, preferred_eleme...  29.9 us
    slice x12, local copies, waits for them, and re-layouts, pack_lower(): front[t, :, :t + 1, :].reshape(front.shape[1], -1)  12.1 us
    unnamed x2, other arithmetic  11.4 us
  transfers between devices with their start and end apart: 9, of which 5 were waited for; matrix products, arithmetic and copies ran while one was open for 15% of the time, Pallas kernels for 13%

profile of v2, /device:TPU:0, one launch (start us, length us, event | category | flops | bytes accessed | tf_op | source)
XLA Modules:
  0.0 503.0 jit_solution(17013116189550127054)
XLA Ops:
  8.1 11.4 %reduce.4 = f32[7,128,7,128]{3,2,1,0:T(8,128)} reduce(f32[1,7,1,128,7,1,128]{6,5,4,3,2,1,0:T(1,128)} %param.8, f32[]{:T(128)} %constant.268), dimensions={0,2,5}, to_apply=%param.8.reduce_sub_computation | reduce | bytes 6422532 | tf_op args[0]
  30.5 4.7 all-to-all-start
  37.2 3.8 reshape.703
  51.2 4.5 fusion
  55.7 8.0 %all-to-all-start.1 = ((f32[16,4,128,128]{3,2,1,0:T(8,128)}), f32[16,4,128,128]{3,2,1,0:T(8,128)}, u32[]{:S(2)}, u32[]{:S(2)}) async-start(f32[16,4,128,128]{3,2,1,0:T(8,128)} %bitcast.119), calls=%async_computation.1 | async-start | bytes 8388608 | tf_op jit(solution)/shard_map/all_to_all | solution.py:230
  71.2 129.4 %all-gather.7.cloned.1.call-done = f32[1664,512]{1,0:T(8,128)} async-done(((f32[1664,128]{1,0:T(8,128)}), f32[1664,512]{1,0:T(8,128)}) %all-gather.7.cloned.1.call-update) | async-done | bytes 3407888 | tf_op jit(solution)/shard_map/all_gather | solution.py:209
  200.7 3.0 slice_select_fusion
  203.8 33.1 %pivot_factors.2 = (f32[512,512]{1,0:T(8,128)}, f32[512,512]{1,0:T(8,128)}) custom-call(f32[512,512]{1,0:T(8,128)} %copy.124.corner_ref), custom_call_target="tpu_custom_call" | custom-call | flops 8589934592 | bytes 67108864 | tf_op jit(solution)/shard_map/pivot_factors/pallas_call | solution.py:138
  236.8 5.5 %fusion.2 = f32[896,512]{1,0:T(8,128)} fusion(f32[512,512]{1,0:T(8,128)} %get-tuple-element.19, f32[1664,512]{1,0:T(8,128)S(1)} %copy-done.3), kind=kOutput, calls=%fused_computation.19 | convolution fusion | flops 2818572288 | bytes 4718592 | tf_op jit(solution)/shard_map/ik,jk->ij/dot_general | solution.py:152
  242.4 7.6 %all-reduce.8.cloned.1.call-done = f32[896,512]{1,0:T(8,128)} async-done(((f32[896,512]{1,0:T(8,128)}), f32[896,512]{1,0:T(8,128)}) %all-reduce.8.cloned.1.call-update) | async-done | bytes 1835024 | tf_op jit(solution)/shard_map/psum | solution.py:15
  249.9 6.2 %fusion.25 = f32[896,512]{1,0:T(8,128)} fusion(f32[896,512]{1,0:T(8,128)} %all-reduce.8.cloned.1.call-done, f32[512,512]{1,0:T(8,128)} %get-tuple-element.19), kind=kOutput, calls=%fused_computation.143 | convolution fusion | flops 2818572288 | bytes 4718592 | tf_op jit(solution)/shard_map/ik,jk->ij/dot_general | solution.py:152
  256.1 4.7 copy.137
  260.8 4.8 gather_fusion.4
  265.5 4.4 broadcast_select_fusion
  275.1 3.9 bitcast_subtract_fusion
  281.0 3.2 copy_add_fusion
  313.3 38.2 %collective-permute-done = f32[128,3584]{1,0:T(8,128)S(1)} collective-permute-done((f32[128,3584]{1,0:T(8,128)S(1)}, f32[128,3584]{1,0:T(8,128)S(1)}, u32[]{:S(2)}, u32[]{:S(2)}) %collective-permute-start) | collective-permute-done | bytes 1835040 | tf_op jit(solution)/shard_map/ppermute | solution.py:25
  358.3 33.4 %all-gather.13.cloned.1.call-done = f32[2048,128]{1,0:T(8,128)} async-done(((f32[128,128]{1,0:T(8,128)}), f32[2048,128]{1,0:T(8,128)}) %all-gather.13.cloned.1.call-update) | async-done | bytes 1048592 | tf_op jit(solution)/shard_map/all_gather | solution.py:159
  399.1 2.9 fusion.7.corner_ref
  402.0 33.0 %pivot_factors.3 = (f32[512,512]{1,0:T(8,128)}, f32[512,512]{1,0:T(8,128)}) custom-call(f32[512,512]{1,0:T(8,128)} %fusion.7.corner_ref), custom_call_target="tpu_custom_call" | custom-call | flops 8589934592 | bytes 67108864 | tf_op jit(solution)/shard_map/pivot_factors/pallas_call | solution.py:138
  435.0 6.0 %broadcast_select_fusion.2 = (f32[768,512]{1,0:T(8,128)}, f32[768,512]{1,0:T(8,128)}) fusion(pred[]{:T(512)S(6)} %eq.246, f32[768,512]{1,0:T(8,128)} %all-gather.9.cloned.1.call-done, f32[512,512]{1,0:T(8,128)} %get-tuple-element.21), kind=kOutput, calls=%fused_computation.34 | convolution fusion | flops 2416312320 | bytes 5767169 | tf_op jit(solution)/shard_map/ik,jk->ij/dot_general | solution.py:152
  449.5 33.4 %all-reduce.10.cloned.1.call-done = f32[768,512]{1,0:T(8,128)} async-done(((f32[768,512]{1,0:T(8,128)}), f32[768,512]{1,0:T(8,128)}) %all-reduce.10.cloned.1.call-update) | async-done | bytes 1572880 | tf_op jit(solution)/shard_map/psum | solution.py:15
  482.9 5.5 %slice_subtract_fusion = f32[768,768]{1,0:T(8,128)} fusion(f32[896,896]{1,0:T(8,128)S(1)} %bitcast_add_fusion, f32[768,512]{1,0:T(8,128)} %get-tuple-element.53, f32[768,512]{1,0:T(8,128)} %all-reduce.10.cloned.1.call-done), kind=kOutput, calls=%fused_computation.15 | convolution fusion | flops 1812529152 | bytes 7864320 | tf_op jit(solution)/shard_map/ik,jk->ij/dot_general | solution.py:152
  492.1 3.8 copy.157
  (183 shorter events, 93.8 us)
Async XLA Ops:
  7.2 16.6 %copy-start = (s32[1,2,24]{2,1,0:T(2,128)S(1)}, s32[1,2,24]{2,1,0:T(2,128)}, u32[]{:S(2)}) copy-start(s32[1,2,24]{2,1,0:T(2,128)} %param.13) | copy-start | bytes 580
  7.2 60.2 %all-gather.11.cloned.1.call-start = ((), (), s32[]{:S(2)}) async-start(), calls=%async_computation.6 | async-start | bytes 1114112 | tf_op jit(solution)/shard_map/all_gather | solution.py:159
  19.5 2.0 copy-start.2
  30.5 25.2 %all-to-all-start = ((f32[4,2,128,128]{3,2,1,0:T(8,128)}), f32[4,2,128,128]{3,2,1,0:T(8,128)}, u32[]{:S(2)}, u32[]{:S(2)}) async-start(f32[4,2,128,128]{3,2,1,0:T(8,128)} %select_multiply_fusion), calls=%async_computation | async-start | bytes 1048576 | tf_op jit(solution)/shard_map/all_to_all | solution.py:201
  55.7 9.9 %copy-start.6 = (f32[768,128]{1,0:T(8,128)S(1)}, f32[768,128]{1,0:T(8,128)}, u32[]{:S(2)}) copy-start(f32[768,128]{1,0:T(8,128)} %slice.135) | copy-start | bytes 1179652
  55.7 200.4 %all-to-all-start.1 = ((f32[16,4,128,128]{3,2,1,0:T(8,128)}), f32[16,4,128,128]{3,2,1,0:T(8,128)}, u32[]{:S(2)}, u32[]{:S(2)}) async-start(f32[16,4,128,128]{3,2,1,0:T(8,128)} %bitcast.119), calls=%async_computation.1 | async-start | bytes 8388608 | tf_op jit(solution)/shard_map/all_to_all | solution.py:230
  63.7 3.0 copy-start.10
  63.7 3.0 copy-start.9
  63.7 137.0 %all-gather.7.cloned.1.call-start = ((), (), s32[]{:S(2)}) async-start(), calls=%async_computation.2 | async-start | bytes 4259840 | tf_op jit(solution)/shard_map/all_gather | solution.py:209
  66.6 183.4 %all-reduce.8.cloned.1.call-start = ((), (), s32[]{:S(2)}) async-start(), calls=%async_computation.3 | async-start | bytes 3670016 | tf_op jit(solution)/shard_map/psum | solution.py:15
  203.7 33.1 %copy-start.3 = (f32[1664,512]{1,0:T(8,128)S(1)}, f32[1664,512]{1,0:T(8,128)}, u32[]{:S(2)}) copy-start(f32[1664,512]{1,0:T(8,128)} %all-gather.7.cloned.1.call-done) | copy-start | bytes 10223620
  203.7 188.0 %all-gather.13.cloned.1.call-start = ((), (), s32[]{:S(2)}) async-start(), calls=%async_computation.7 | async-start | bytes 1114112 | tf_op jit(solution)/shard_map/all_gather | solution.py:159
  273.0 1.9 copy-start.4
  273.0 2.0 copy-start.5
  281.0 3.2 copy-start.8
  309.9 41.7 %copy-start.11 = (pred[896]{0:T(1024)(128)(4,1)S(1)}, pred[896]{0:T(1024)(128)(4,1)}, u32[]{:S(2)}) copy-start(pred[896]{0:T(1024)(128)(4,1)} %constant.253.clone.1) | copy-start | bytes 2692
  309.9 41.7 %collective-permute-start = (f32[128,3584]{1,0:T(8,128)S(1)}, f32[128,3584]{1,0:T(8,128)S(1)}, u32[]{:S(2)}, u32[]{:S(2)}) collective-permute-start(f32[128,3584]{1,0:T(8,128)S(1)} %constant_dynamic-update-slice_fusion), channel_id=1, source_target_pairs={{0,16},{16,0},{1,17},{17,1},{2,18},{18,2},{3,19},{19,3},{4,20},{20... | collective-permute-start | bytes 5505032 | tf_op jit(solution)/shard_map/ppermute | solution.py:25
  353.6 81.4 %all-gather.9.cloned.1.call-start = ((), (), s32[]{:S(2)}) async-start(), calls=%async_computation.4 | async-start | bytes 1966080 | tf_op jit(solution)/shard_map/all_gather | solution.py:178
  354.5 128.5 %all-reduce.10.cloned.1.call-start = ((), (), s32[]{:S(2)}) async-start(), calls=%async_computation.5 | async-start | bytes 3145728 | tf_op jit(solution)/shard_map/psum | solution.py:15
  357.4 41.8 %copy-start.7 = (pred[512,512]{0,1:T(8,128)(4,1)S(1)}, pred[512,512]{0,1:T(8,128)(4,1)}, u32[]{:S(2)}) copy-start(pred[512,512]{0,1:T(8,128)(4,1)} %copy.152) | copy-start | bytes 786436
  490.9 5.0 %copy-start.1 = (s32[1,2,24]{2,1,0:T(2,128)S(1)}, s32[1,2,24]{2,1,0:T(2,128)}, u32[]{:S(2)}) copy-start(s32[1,2,24]{2,1,0:T(2,128)} %param.13) | copy-start | bytes 580
Sparse Core Ops, SparseCore 0:
  23.8 40.6 all-gather.10
  66.7 133.9 all-gather.6
  203.9 46.0 all-reduce.7
  353.7 37.9 all-gather.12
  393.7 36.6 all-gather.8
  441.1 41.7 all-reduce.9
